TPU v7x, 256 devices: a whole 4x4x8 slice. The times are simulated.
256 devices in a mesh: tm: 16 (over x_hi, z), tensor: 16 (over x_lo, y, core).
Axes of the slice: x: 4 (x_hi: 2, x_lo: 2; x = x_hi * 2 + x_lo), y: 4, z: 8, core: 2. Of those that a mesh axis runs over, the one named last changes fastest.
Arguments:
- features: bfloat16 [2, 2048, 1536], P(None, 'tm'), may hold values from -6 to 6
- lengths: int32 [2], replicated, may hold values from 512 to 2048, as said below
- norm_gains: float32 [2, 1536], replicated, may hold values from 0.1 to 1.9
- qkv_weight: bfloat16 [3, 1536, 1536], P(None, 'tensor'), may hold values from -0.21650635 to 0.21650635
- pos_weight: bfloat16 [1536, 1536], P('tensor'), may hold values from -0.15625 to 0.15625
- pos_biases: float32 [2, 1536], P(None, 'tensor'), may hold values from -3 to 3
- out_weight: bfloat16 [1536, 1536], P('tensor'), may hold values from -0.15625 to 0.15625
- conv_in_weight: bfloat16 [2, 1536, 1536], P(None, 'tensor'), may hold values from -0.15625 to 0.15625
- depth_kernel: float32 [31, 1536], P(None, 'tensor'), may hold values from -1 to 1
- conv_scale: float32 [1536], P('tensor'), may hold values from 0.1 to 1.9
- conv_shift: float32 [1536], P('tensor'), may hold values from -3 to 3
- conv_out_weight: bfloat16 [1536, 1536], P('tensor'), may hold values from -0.15625 to 0.15625
Outputs:
- encoded: bfloat16 [2, 2048, 1536], P(None, ('tm', 'tensor'))
Inputs may be any that keep to these rules, and one draw needn't show every extreme that they name: `lengths`: the first window is whole.
All inputs are finite; a program needn't handle non-finite values.
Results may differ from a plain program's by a relative error of at most 0.017.
Values may be sent and summed in bfloat16 or wider, within the bound.
A program may use at most 64 MiB of HBM per device.

v0:
```python
import math
import jax
import jax.numpy as jnp
from jax import lax
from jax.sharding import PartitionSpec as P

HD = 96
epsilon = 1e-05


def padded_2(cells, sides, width):
    for axis, dim in sides:
        count = lax.axis_size(axis)
        ends = count - 1
        head = lax.slice_in_dim(cells, 0, width, axis=dim)
        tail = lax.slice_in_dim(cells, cells.shape[dim] - width, cells.shape[dim], axis=dim)
        cells = jnp.concatenate(
            [
                lax.ppermute(tail, axis, [(i, (i + 1) % count) for i in range(ends)]),
                cells,
                lax.ppermute(head, axis, [((i + 1) % count, i) for i in range(ends)]),
            ],
            axis=dim,
        )
    return cells


def layer_norm(values, gain):
    values = values.astype(jnp.float32)
    row_mean = jnp.mean(values, axis=-1, keepdims=True)
    centred = values - row_mean
    variance = jnp.mean(centred * centred, axis=-1, keepdims=True)
    return centred * lax.rsqrt(variance + epsilon) * gain


def positions(offsets, model_width, pos_weight):
    half_width = model_width // 2
    frequency = jnp.exp(
        jnp.arange(half_width, dtype=jnp.float32) * (-2.0 * math.log(10000.0) / model_width)
    )
    angles = offsets.astype(jnp.float32)[:, None] * frequency[None, :]
    pos_table = jnp.concatenate(
        [jnp.sin(angles).astype(jnp.bfloat16), jnp.cos(angles).astype(jnp.bfloat16)], axis=1
    )
    return jnp.einsum(
        "md,cd->mc", pos_table, pos_weight, preferred_element_type=jnp.float32
    ).astype(jnp.bfloat16)


def diagonal_take(pos_table, row_count, col_count):
    table_width = pos_table.shape[-1]
    leading = pos_table.shape[:-2]
    flattened = pos_table.reshape(leading + (row_count * table_width,))
    flattened = lax.slice_in_dim(
        flattened,
        row_count - 1,
        row_count - 1 + row_count * (table_width - 1),
        axis=flattened.ndim - 1,
    )
    return flattened.reshape(leading + (row_count, table_width - 1))[..., :col_count]


def shards(
    features,
    lengths,
    norm_gains,
    qkv_weight,
    pos_weight,
    pos_biases,
    out_weight,
    conv_in_weight,
    depth_kernel,
    conv_scale,
    conv_shift,
    conv_out_weight,
):
    windows, local_rows, model_width = features.shape
    channels = qkv_weight.shape[1]
    heads_here = channels // HD
    score_scale = 1.0 / math.sqrt(HD)
    first_frame = lax.axis_index("tm") * local_rows
    frame_ids = first_frame + jnp.arange(local_rows, dtype=jnp.int32)
    normed = layer_norm(features, norm_gains[0]).astype(jnp.bfloat16)
    projections = jnp.einsum(
        "btd,gcd->btgc", normed, qkv_weight, preferred_element_type=jnp.float32
    )
    query_all = projections[:, :, 0]
    content_q = (
        (query_all + pos_biases[0])
        .astype(jnp.bfloat16)
        .reshape(windows, local_rows, heads_here, HD)
    )
    position_q = (
        (query_all + pos_biases[1])
        .astype(jnp.bfloat16)
        .reshape(windows, local_rows, heads_here, HD)
    )
    key_rows = projections[:, :, 1].astype(jnp.bfloat16)
    value_rows = projections[:, :, 2].astype(jnp.bfloat16)
    global_frames = local_rows * lax.axis_size("tm")
    table_rows = global_frames + local_rows - 1
    all_offsets = first_frame + local_rows - 1 - jnp.arange(table_rows, dtype=jnp.int32)
    relative_all = positions(all_offsets, model_width, pos_weight).reshape(
        table_rows, heads_here, HD
    )
    running_max = jnp.full((windows, heads_here, local_rows), -1e30, jnp.float32)
    key_piece = lax.all_gather(key_rows, "tm", axis=1, tiled=True)
    value_piece = lax.all_gather(value_rows, "tm", axis=1, tiled=True)
    key_count = key_piece.shape[1]
    key_heads = key_piece.reshape(windows, key_count, heads_here, HD)
    value_heads = value_piece.reshape(windows, key_count, heads_here, HD)
    content_scores = jnp.einsum(
        "bqhe,bkhe->bhqk", content_q, key_heads, preferred_element_type=jnp.float32
    )
    full_pos = jnp.einsum(
        "bqhe,mhe->bhqm", position_q, relative_all, preferred_element_type=jnp.float32
    )
    scores = (content_scores + diagonal_take(full_pos, local_rows, key_count)) * score_scale
    key_ids = jnp.arange(key_count, dtype=jnp.int32)
    key_mask = (key_ids[None, :] < lengths[:, None])[:, None, None, :]
    scores = jnp.where(key_mask, scores, -1e30)
    new_max = jnp.maximum(running_max, jnp.max(scores, axis=-1))
    attention_weights = jnp.where(key_mask, jnp.exp(scores - new_max[..., None]), 0.0)
    running_sum = jnp.sum(attention_weights, axis=-1)
    weighted = jnp.einsum(
        "bhqk,bkhe->bhqe",
        attention_weights.astype(jnp.bfloat16),
        value_heads,
        preferred_element_type=jnp.float32,
    )
    head_outputs = (weighted / running_sum[..., None]).astype(jnp.bfloat16)
    head_outputs = head_outputs.transpose(0, 2, 1, 3).reshape(windows, local_rows, channels)
    attention_term = jnp.einsum(
        "btc,cd->btd", head_outputs, out_weight, preferred_element_type=jnp.float32
    )
    row_count = local_rows // lax.axis_size("tensor")
    row_start = lax.axis_index("tensor") * row_count
    attention_full = lax.psum(attention_term.astype(jnp.bfloat16), "tensor").astype(jnp.float32)
    hidden = (features.astype(jnp.float32) + attention_full).astype(jnp.bfloat16)
    hidden_rows = lax.dynamic_slice_in_dim(hidden, row_start, row_count, 1)
    normed_two = layer_norm(hidden, norm_gains[1]).astype(jnp.bfloat16)
    widened = jnp.einsum(
        "btd,gcd->btgc", normed_two, conv_in_weight, preferred_element_type=jnp.float32
    )
    gated_units = widened[:, :, 0] * jax.nn.sigmoid(widened[:, :, 1])
    frame_valid = frame_ids[None, :] < lengths[:, None]
    gated_units = jnp.where(frame_valid[:, :, None], gated_units, 0.0).astype(jnp.bfloat16)
    rim = depth_kernel.shape[0] // 2
    padded = padded_2(gated_units, (("tm", 1),), rim)
    depth_sum = jnp.zeros(gated_units.shape, jnp.float32)
    for tap_index in range(depth_kernel.shape[0]):
        depth_sum = (
            depth_sum
            + padded[:, tap_index : tap_index + local_rows].astype(jnp.float32)
            * depth_kernel[tap_index]
        )
    affine = depth_sum * conv_scale + conv_shift
    activated = (affine * jax.nn.sigmoid(affine)).astype(jnp.bfloat16)
    conv_term = jnp.einsum(
        "btc,cd->btd", activated, conv_out_weight, preferred_element_type=jnp.float32
    )
    conv_rows = lax.psum_scatter(
        conv_term.astype(jnp.bfloat16), "tensor", scatter_dimension=1, tiled=True
    ).astype(jnp.float32)
    return (hidden_rows.astype(jnp.float32) + conv_rows).astype(jnp.bfloat16)


def solution(mesh):
    return jax.shard_map(
        shards,
        mesh=mesh,
        in_specs=(
            P(None, "tm", None),
            P(),
            P(),
            P(None, "tensor", None),
            P("tensor", None),
            P(None, "tensor"),
            P("tensor", None),
            P(None, "tensor", None),
            P(None, "tensor"),
            P("tensor"),
            P("tensor"),
            P("tensor", None),
        ),
        out_specs=P(None, ("tm", "tensor"), None),
        check_vma=False,
    )
```

profile of v0, /device:TPU:4, one launch (start us, length us, event | category | flops | bytes accessed | tf_op | source)
XLA Modules:
  0.0 364.2 jit_solution(17981048727000011265)
XLA Ops:
  6.5 0.8 slice_reduce_fusion
  7.4 1.3 convert_reduce_fusion
  8.7 1.5 fusion.21
  10.2 0.8 slice_bitcast_fusion.32
  11.0 26.0 %fusion = (bf16[2175,768]{1,0:T(8,128)(2,1)}, bf16[2175,768]{1,0:T(8,128)(2,1)}) fusion(f32[768]{0:T(1024)S(1)} %multiply_exponential_fusion, f32[2175]{0:T(1024)S(1)} %subtract_convert_fusion), kind=kLoop, calls=%fused_computation.2 | loop fusion | flops 5011200 | bytes 6693372 | tf_op jit(solution)/shard_map/convert_element_type | solution.py:43
  38.3 6.8 %convolution_bitcast_fusion = f32[2,1,128,2175]{2,3,0,1:T(8,128)} fusion(bf16[96,1536]{1,0:T(8,128)(2,1)S(1)} %copy-done.7, bf16[2175,768]{1,0:T(8,128)(2,1)} %get-tuple-element.45, bf16[2175,768]{1,0:T(8,128)(2,1)} %get-tuple-element.44, f32[2,128,3,96]{1,3,2,0:T(8,128)S(1)} %get-tuple-element.49, f32[96]{0:T(128)S(1)} %get-tuple-element.47), kind=kOutput, calls=%fused_computation.8 | convolution fusion | flops 761960320 | bytes 9302528 | tf_op jit(solution)/shard_map/bqhe,mhe->bhqm/dot_general | solution.py:115
  45.1 2.0 copy.14
  47.1 4.4 %reshape.176 = f32[2,1,278400]{2,0,1:T(2,128)} reshape(f32[2,1,128,2175]{3,2,0,1:T(8,128)S(1)} %copy.14) | data formatting | bytes 4454400 | tf_op jit(solution)/shard_map/reshape | solution.py:53
  51.5 3.9 %slice.330 = f32[2,1,278272]{2,0,1:T(2,128)S(1)} slice(f32[2,1,278400]{2,0,1:T(2,128)} %reshape.176), slice={[0:2], [0:1], [127:278399]} | slice | bytes 4452352 | tf_op jit(solution)/shard_map/slice | solution.py:54
  55.5 4.5 %reshape.177 = f32[2,1,128,2174]{3,2,0,1:T(8,128)} reshape(f32[2,1,278272]{2,0,1:T(2,128)S(1)} %slice.330) | data formatting | bytes 4452352 | tf_op jit(solution)/shard_map/reshape | solution.py:60
  59.9 46.0 %all-gather = bf16[2,2048,1,96]{1,3,2,0:T(8,128)(2,1)S(1)} all-gather(bf16[2,128,1,96]{1,3,2,0:T(8,128)(2,1)S(1)} %get-tuple-element.10), channel_id=2, replica_groups=mesh['tm'=16,'tensor'=16] {'tm'}, dimensions={1}, use_global_device_ids=true | all-gather | bytes 835584 | tf_op jit(solution)/shard_map/all_gather | solution.py:107
  106.0 2.4 fusion.172
  108.4 42.4 %all-gather.1 = bf16[2,2048,1,96]{1,3,2,0:T(8,128)(2,1)} all-gather(bf16[2,128,1,96]{1,3,2,0:T(8,128)(2,1)S(1)} %get-tuple-element.9), channel_id=3, replica_groups=mesh['tm'=16,'tensor'=16] {'tm'}, dimensions={1}, use_global_device_ids=true | all-gather | bytes 835584 | tf_op jit(solution)/shard_map/all_gather | solution.py:108
  151.4 2.9 convolution_convert_fusion.1
  154.5 122.0 %all-reduce.2.cloned.1.call-done = bf16[2,128,1536]{2,1,0:T(8,128)(2,1)} async-done(((bf16[2,128,1536]{2,1,0:T(8,128)(2,1)}), bf16[2,128,1536]{2,1,0:T(8,128)(2,1)}) %all-reduce.2.cloned.1.call-update) | async-done | bytes 786448 | tf_op jit(solution)/shard_map/psum | solution.py:138
  276.4 1.7 convert_reduce_fusion.1
  279.2 3.5 collective-permute-start
  282.7 6.0 %collective-permute-start.1 = (bf16[2,15,96]{1,2,0:T(8,128)(2,1)S(1)}, bf16[2,15,96]{1,2,0:T(8,128)(2,1)S(1)}, u32[]{:S(2)}, u32[]{:S(2)}) collective-permute-start(bf16[2,15,96]{1,2,0:T(8,128)(2,1)S(1)} %get-tuple-element.12), channel_id=1, source_target_pairs={{16,0},{32,16},{48,32},{64,48},{80,64},{96,80},{112,96},{128,112},... | collective-permute-start | bytes 17288 | tf_op jit(solution)/shard_map/ppermute | solution.py:21
  288.8 1.6 collective-permute-done.1
  290.4 1.7 convolution_convert_fusion
  292.1 0.8 copy.17
  292.9 1.0 copy.19
  293.9 62.0 %reduce-scatter.4.cloned.1.call-done = bf16[8,3072]{1,0:T(8,128)(2,1)} async-done(((bf16[128,3072]{1,0:T(8,128)(2,1)}), bf16[8,3072]{1,0:T(8,128)(2,1)}) %reduce-scatter.4.cloned.1.call-update) | async-done | bytes 49168
  355.9 0.8 reshape.190
  (47 shorter events, 3.9 us)
Async XLA Ops:
  6.5 30.5 %copy-start = (bf16[3,96,1536]{2,1,0:T(8,128)(2,1)S(1)}, bf16[3,96,1536]{2,1,0:T(8,128)(2,1)}, u32[]{:S(2)}) copy-start(bf16[3,96,1536]{2,1,0:T(8,128)(2,1)} %param.15) | copy-start | bytes 2654212
  6.5 269.9 %all-reduce.2.cloned.1.call-start = ((), (), s32[]{:S(2)}) async-start(), calls=%async_computation.1 | async-start | bytes 1572864 | tf_op jit(solution)/shard_map/psum | solution.py:138
  11.0 26.0 %copy-start.1 = (bf16[2,128,1536]{2,1,0:T(8,128)(2,1)S(1)}, bf16[2,128,1536]{2,1,0:T(8,128)(2,1)}, u32[]{:S(2)}) copy-start(bf16[2,128,1536]{2,1,0:T(8,128)(2,1)} %param.12) | copy-start | bytes 2359300
  37.0 1.3 copy-start.7
  37.6 0.7 copy-start.3
  55.4 50.5 %copy-start.5 = (s32[2]{0:T(128)S(1)}, s32[2]{0:T(128)}, u32[]{:S(2)}) copy-start(s32[2]{0:T(128)} %param.13) | copy-start | bytes 28
  108.4 43.0 %copy-start.2 = (bf16[96,1536]{1,0:T(8,128)(2,1)S(1)}, bf16[96,1536]{1,0:T(8,128)(2,1)}, u32[]{:S(2)}) copy-start(bf16[96,1536]{1,0:T(8,128)(2,1)} %param.18) | copy-start | bytes 884740
  151.4 3.1 copy-start.4
  154.3 124.2 %copy-start.6 = (bf16[2,96,1536]{2,1,0:T(8,128)(2,1)S(1)}, bf16[2,96,1536]{2,1,0:T(8,128)(2,1)}, u32[]{:S(2)}) copy-start(bf16[2,96,1536]{2,1,0:T(8,128)(2,1)} %param.19) | copy-start | bytes 1769476
  154.3 201.6 %reduce-scatter.4.cloned.1.call-start = ((), (), s32[]{:S(2)}) async-start(), calls=%async_computation.2 | async-start | bytes 835584
  278.1 12.3 %copy-start.8 = (bf16[96,1536]{1,0:T(8,128)(2,1)S(1)}, bf16[96,1536]{1,0:T(8,128)(2,1)}, u32[]{:S(2)}) copy-start(bf16[96,1536]{1,0:T(8,128)(2,1)} %param.23) | copy-start | bytes 884740
  278.1 12.3 %copy-start.9 = (f32[96]{0:T(128)S(1)}, f32[96]{0:T(128)}, u32[]{:S(2)}) copy-start(f32[96]{0:T(128)} %param.22) | copy-start | bytes 1156
  278.1 12.3 %copy-start.10 = (f32[96]{0:T(128)S(1)}, f32[96]{0:T(128)}, u32[]{:S(2)}) copy-start(f32[96]{0:T(128)} %param.21) | copy-start | bytes 1156
  279.2 9.6 %collective-permute-start = (bf16[2,15,96]{1,2,0:T(8,128)(2,1)S(1)}, bf16[2,15,96]{1,2,0:T(8,128)(2,1)S(1)}, u32[]{:S(2)}, u32[]{:S(2)}) collective-permute-start(bf16[2,15,96]{1,2,0:T(8,128)(2,1)S(1)} %get-tuple-element.11), channel_id=1, source_target_pairs={{0,16},{16,32},{32,48},{48,64},{64,80},{80,96},{96,112},{112,128},... | collective-permute-start | bytes 17288 | tf_op jit(solution)/shard_map/ppermute | solution.py:19
  282.7 7.7 %collective-permute-start.1 = (bf16[2,15,96]{1,2,0:T(8,128)(2,1)S(1)}, bf16[2,15,96]{1,2,0:T(8,128)(2,1)S(1)}, u32[]{:S(2)}, u32[]{:S(2)}) collective-permute-start(bf16[2,15,96]{1,2,0:T(8,128)(2,1)S(1)} %get-tuple-element.12), channel_id=1, source_target_pairs={{16,0},{32,16},{48,32},{64,48},{80,64},{96,80},{112,96},{128,112},... | collective-permute-start | bytes 17288 | tf_op jit(solution)/shard_map/ppermute | solution.py:21
Sparse Core Ops, SparseCore 0:
  154.4 121.9 all-reduce.1
  294.0 61.8 reduce-scatter.3
where the time goes:
time: 365 us; the launch traced here: 364 us
  waiting for transfers between devices  186 us (51%)
  blocking collectives  88.5 us (24%)
  other arithmetic  32.2 us (9%)
  local copies, waits for them, and re-layouts  19.9 us (5%)
  matrix products  14.8 us (4%)
  between operations  13.6 us (4%)
  starting transfers between devices  9.5 us (3%)
    psum x1, waiting for transfers between devices, shards(): lax.psum(attention_term.astype(jnp.bfloat16), 'tensor').astype(jnp.float32)  122 us
    unnamed x3, waiting for transfers between devices  62 us
    all_gather x1, blocking collectives, shards(): key_piece = lax.all_gather(key_rows, 'tm', axis=1, tiled=True)  46 us
    all_gather x1, blocking collectives, shards(): value_piece = lax.all_gather(value_rows, 'tm', axis=1, tiled=True)  42.4 us
    convert_element_type x1, other arithmetic, positions(): jnp.sin(angles).astype(jnp.bfloat16)  26 us
  transfers between devices with their start and end apart: 4, of which 4 were waited for; matrix products, arithmetic and copies ran while one was open for 0% of the time, Pallas kernels for 0%

commit v1 on v0

--- a/solution.py
+++ b/solution.py
@@ -104,8 +104,11 @@
         table_rows, heads_here, HD
     )
     running_max = jnp.full((windows, heads_here, local_rows), -1e30, jnp.float32)
-    key_piece = lax.all_gather(key_rows, "tm", axis=1, tiled=True)
-    value_piece = lax.all_gather(value_rows, "tm", axis=1, tiled=True)
+    key_piece, value_piece = jnp.split(
+        lax.all_gather(jnp.concatenate([key_rows, value_rows], axis=0), "tm", axis=1, tiled=True),
+        [key_rows.shape[0]],
+        axis=0,
+    )
     key_count = key_piece.shape[1]
     key_heads = key_piece.reshape(windows, key_count, heads_here, HD)
     value_heads = value_piece.reshape(windows, key_count, heads_here, HD)

time: 365 us -> 310 us (0.85)
  blocking collectives: 88.5 us -> 0 us
  waiting for transfers between devices: 186 us -> 219 us
    all_gather x2 -> x0, blocking collectives: 88.5 us -> none  [the longest x1 46 us: shards(): key_piece = lax.all_gather(key_rows, 'tm', axis=1, tiled=True)]
    all_gather x0 -> x1, waiting for transfers between devices: none -> 33 us  [shards(): lax.all_gather(jnp.concatenate([key_rows, value_rows], axis=0), 'tm', axi...]
    unnamed x3 -> x4, waiting for transfers between devices: 62 us -> 62 us
  transfers between devices with their start and end apart: 4 -> 5, of which waited for: 4 -> 5; matrix products, arithmetic and copies ran while one was open for 0% -> 15% of each run, Pallas kernels for 0% -> 0%
where the time goes in v1:
time: 310 us
  waiting for transfers between devices  219 us (71%)
  other arithmetic  33 us (11%)
  local copies, waits for them, and re-layouts  18.8 us (6%)
  matrix products  16.2 us (5%)
  between operations  13.4 us (4%)
  starting transfers between devices  9.72 us (3%)
    psum x1, waiting for transfers between devices, shards(): lax.psum(attention_term.astype(jnp.bfloat16), 'tensor').astype(jnp.float32)  122 us
    unnamed x4, waiting for transfers between devices  62 us
    all_gather x1, waiting for transfers between devices, shards(): lax.all_gather(jnp.concatenate([key_rows, value_rows], axis=0), 'tm', axi...  33 us
    convert_element_type x1, other arithmetic, positions(): jnp.sin(angles).astype(jnp.bfloat16)  26 us
    dot_general x1, matrix products, shards(): jnp.einsum('bqhe,mhe->bhqm', position_q, relative_all, preferred_element_...  6.83 us
  transfers between devices with their start and end apart: 5, of which 5 were waited for; matrix products, arithmetic and copies ran while one was open for 15% of the time, Pallas kernels for 0%

profile of v1, /device:TPU:4, one launch (start us, length us, event | category | flops | bytes accessed | tf_op | source)
XLA Modules:
  0.0 310.0 jit_solution(13718630089570766026)
XLA Ops:
  6.5 0.8 slice_reduce_fusion
  7.4 1.3 convert_reduce_fusion
  8.7 1.5 fusion.21
  10.2 1.7 fusion.170
  11.9 0.7 pad_maximum_fusion
  12.8 26.0 %fusion = (bf16[2175,768]{1,0:T(8,128)(2,1)}, bf16[2175,768]{1,0:T(8,128)(2,1)}) fusion(f32[768]{0:T(1024)S(1)} %multiply_exponential_fusion, f32[2175]{0:T(1024)S(1)} %subtract_convert_fusion), kind=kLoop, calls=%fused_computation.2 | loop fusion | flops 5011200 | bytes 6693372 | tf_op jit(solution)/shard_map/convert_element_type | solution.py:43
  38.9 6.8 %convolution_bitcast_fusion = f32[2,1,128,2175]{2,3,0,1:T(8,128)} fusion(bf16[96,1536]{1,0:T(8,128)(2,1)S(1)} %copy-done.7, bf16[2175,768]{1,0:T(8,128)(2,1)} %get-tuple-element.45, bf16[2175,768]{1,0:T(8,128)(2,1)} %get-tuple-element.44, f32[2,128,3,96]{1,3,2,0:T(8,128)S(1)} %get-tuple-element.49, f32[96]{0:T(128)S(1)} %get-tuple-element.47), kind=kOutput, calls=%fused_computation.8 | convolution fusion | flops 761960320 | bytes 9302528 | tf_op jit(solution)/shard_map/bqhe,mhe->bhqm/dot_general | solution.py:118
  45.7 2.0 copy.17
  47.7 4.4 %reshape.176 = f32[2,1,278400]{2,0,1:T(2,128)} reshape(f32[2,1,128,2175]{3,2,0,1:T(8,128)S(1)} %copy.17) | data formatting | bytes 4454400 | tf_op jit(solution)/shard_map/reshape | solution.py:53
  52.1 3.9 %slice.331 = f32[2,1,278272]{2,0,1:T(2,128)S(1)} slice(f32[2,1,278400]{2,0,1:T(2,128)} %reshape.176), slice={[0:2], [0:1], [127:278399]} | slice | bytes 4452352 | tf_op jit(solution)/shard_map/slice | solution.py:54
  56.0 4.5 %reshape.177 = f32[2,1,128,2174]{3,2,0,1:T(8,128)} reshape(f32[2,1,278272]{2,0,1:T(2,128)S(1)} %slice.331) | data formatting | bytes 4452352 | tf_op jit(solution)/shard_map/reshape | solution.py:60
  60.5 33.0 %all-gather.2.cloned.1.call-done = bf16[4,2048,96]{1,2,0:T(8,128)(2,1)} async-done(((bf16[4,128,96]{1,2,0:T(8,128)(2,1)}), bf16[4,2048,96]{1,2,0:T(8,128)(2,1)}) %all-gather.2.cloned.1.call-update) | async-done | bytes 1572880 | tf_op jit(solution)/shard_map/all_gather | solution.py:108
  93.6 2.6 fusion.171
  97.1 2.9 convolution_convert_fusion.1
  100.4 122.1 %all-reduce.2.cloned.1.call-done = bf16[2,128,1536]{2,1,0:T(8,128)(2,1)} async-done(((bf16[2,128,1536]{2,1,0:T(8,128)(2,1)}), bf16[2,128,1536]{2,1,0:T(8,128)(2,1)}) %all-reduce.2.cloned.1.call-update) | async-done | bytes 786448 | tf_op jit(solution)/shard_map/psum | solution.py:141
  222.5 1.7 convert_reduce_fusion.1
  225.3 3.5 %collective-permute-start = (bf16[2,15,96]{1,2,0:T(8,128)(2,1)S(1)}, bf16[2,15,96]{1,2,0:T(8,128)(2,1)S(1)}, u32[]{:S(2)}, u32[]{:S(2)}) collective-permute-start(bf16[2,15,96]{1,2,0:T(8,128)(2,1)S(1)} %get-tuple-element.11), channel_id=1, source_target_pairs={{0,16},{16,32},{32,48},{48,64},{64,80},{80,96},{96,112},{112,128},... | collective-permute-start | bytes 17288 | tf_op jit(solution)/shard_map/ppermute | solution.py:19
  228.8 6.0 %collective-permute-start.1 = (bf16[2,15,96]{1,2,0:T(8,128)(2,1)S(1)}, bf16[2,15,96]{1,2,0:T(8,128)(2,1)S(1)}, u32[]{:S(2)}, u32[]{:S(2)}) collective-permute-start(bf16[2,15,96]{1,2,0:T(8,128)(2,1)S(1)} %get-tuple-element.12), channel_id=1, source_target_pairs={{16,0},{32,16},{48,32},{64,48},{80,64},{96,80},{112,96},{128,112},... | collective-permute-start | bytes 17288 | tf_op jit(solution)/shard_map/ppermute | solution.py:21
  234.9 1.6 collective-permute-done.1
  236.5 1.7 convolution_convert_fusion
  238.2 0.8 copy.20
  239.0 1.0 copy.23
  240.0 62.0 %reduce-scatter.4.cloned.1.call-done = bf16[8,3072]{1,0:T(8,128)(2,1)} async-done(((bf16[128,3072]{1,0:T(8,128)(2,1)}), bf16[8,3072]{1,0:T(8,128)(2,1)}) %reduce-scatter.4.cloned.1.call-update) | async-done | bytes 49168
  302.0 0.8 reshape.188
  (49 shorter events, 3.3 us)
Async XLA Ops:
  6.5 3.7 %copy-start = (bf16[3,96,1536]{2,1,0:T(8,128)(2,1)S(1)}, bf16[3,96,1536]{2,1,0:T(8,128)(2,1)}, u32[]{:S(2)}) copy-start(bf16[3,96,1536]{2,1,0:T(8,128)(2,1)} %param.15) | copy-start | bytes 2654212
  6.5 87.0 %all-gather.2.cloned.1.call-start = ((), (), s32[]{:S(2)}) async-start(), calls=%async_computation.1 | async-start | bytes 1671168 | tf_op jit(solution)/shard_map/all_gather | solution.py:108
  8.7 4.1 %copy-start.4 = (f32[2,96]{1,0:T(2,128)S(1)}, f32[2,96]{1,0:T(2,128)}, u32[]{:S(2)}) copy-start(f32[2,96]{1,0:T(2,128)} %param.17) | copy-start | bytes 2308
  11.9 26.9 %copy-start.2 = (f32[2,128,3,96]{1,3,2,0:T(8,128)}, f32[2,128,3,96]{1,3,2,0:T(8,128)S(1)}, u32[]{:S(2)}) copy-start(f32[2,128,3,96]{1,3,2,0:T(8,128)S(1)} %get-tuple-element.49) | copy-start | bytes 884740
  12.7 209.8 %all-reduce.2.cloned.1.call-start = ((), (), s32[]{:S(2)}) async-start(), calls=%async_computation.2 | async-start | bytes 1572864 | tf_op jit(solution)/shard_map/psum | solution.py:141
  12.8 26.1 %copy-start.7 = (bf16[96,1536]{1,0:T(8,128)(2,1)S(1)}, bf16[96,1536]{1,0:T(8,128)(2,1)}, u32[]{:S(2)}) copy-start(bf16[96,1536]{1,0:T(8,128)(2,1)} %param.16) | copy-start | bytes 884740
  56.0 4.5 %copy-start.5 = (s32[2]{0:T(128)S(1)}, s32[2]{0:T(128)}, u32[]{:S(2)}) copy-start(s32[2]{0:T(128)} %param.13) | copy-start | bytes 28
  96.2 1.0 copy-start.1
  97.1 3.3 %copy-start.3 = (f32[31,96]{1,0:T(8,128)S(1)}, f32[31,96]{1,0:T(8,128)}, u32[]{:S(2)}) copy-start(f32[31,96]{1,0:T(8,128)} %param.20) | copy-start | bytes 35716
  100.0 124.6 %copy-start.6 = (bf16[2,96,1536]{2,1,0:T(8,128)(2,1)S(1)}, bf16[2,96,1536]{2,1,0:T(8,128)(2,1)}, u32[]{:S(2)}) copy-start(bf16[2,96,1536]{2,1,0:T(8,128)(2,1)} %param.19) | copy-start | bytes 1769476
  100.1 201.9 %reduce-scatter.4.cloned.1.call-start = ((), (), s32[]{:S(2)}) async-start(), calls=%async_computation.3 | async-start | bytes 835584
  224.2 12.3 %copy-start.8 = (bf16[96,1536]{1,0:T(8,128)(2,1)S(1)}, bf16[96,1536]{1,0:T(8,128)(2,1)}, u32[]{:S(2)}) copy-start(bf16[96,1536]{1,0:T(8,128)(2,1)} %param.23) | copy-start | bytes 884740
  224.2 12.3 %copy-start.9 = (f32[96]{0:T(128)S(1)}, f32[96]{0:T(128)}, u32[]{:S(2)}) copy-start(f32[96]{0:T(128)} %param.22) | copy-start | bytes 1156
  224.2 12.3 %copy-start.10 = (f32[96]{0:T(128)S(1)}, f32[96]{0:T(128)}, u32[]{:S(2)}) copy-start(f32[96]{0:T(128)} %param.21) | copy-start | bytes 1156
  225.3 9.6 %collective-permute-start = (bf16[2,15,96]{1,2,0:T(8,128)(2,1)S(1)}, bf16[2,15,96]{1,2,0:T(8,128)(2,1)S(1)}, u32[]{:S(2)}, u32[]{:S(2)}) collective-permute-start(bf16[2,15,96]{1,2,0:T(8,128)(2,1)S(1)} %get-tuple-element.11), channel_id=1, source_target_pairs={{0,16},{16,32},{32,48},{48,64},{64,80},{80,96},{96,112},{112,128},... | collective-permute-start | bytes 17288 | tf_op jit(solution)/shard_map/ppermute | solution.py:19
  228.8 7.7 %collective-permute-start.1 = (bf16[2,15,96]{1,2,0:T(8,128)(2,1)S(1)}, bf16[2,15,96]{1,2,0:T(8,128)(2,1)S(1)}, u32[]{:S(2)}, u32[]{:S(2)}) collective-permute-start(bf16[2,15,96]{1,2,0:T(8,128)(2,1)S(1)} %get-tuple-element.12), channel_id=1, source_target_pairs={{16,0},{32,16},{48,32},{64,48},{80,64},{96,80},{112,96},{128,112},... | collective-permute-start | bytes 17288 | tf_op jit(solution)/shard_map/ppermute | solution.py:21
Sparse Core Ops, SparseCore 0:
  12.8 80.7 all-gather.1
  100.2 122.2 all-reduce.1
  240.2 61.8 reduce-scatter.3
